TPU v7x, 128 devices: a whole 4x4x4 slice. The times are simulated.
128 devices in a mesh: gx: 16 (over y, z), gy: 8 (over x, core).
Axes of the slice: x: 4, y: 4, z: 4, core: 2. Of those that a mesh axis runs over, the one named last changes fastest.
Arguments:
- features: float32 [2048, 64, 512], P(('gx', 'gy')), may hold values from -6 to 6
- send_pick: int32 [128, 32], P(('gx', 'gy')), may hold values from -1 to 15, as said below
- occupancy: int32 [4096, 512], P(('gx', 'gy')), may hold values from 0 to 1, as said below
- neighbours: int32 [4096, 6], P(('gx', 'gy')), may hold values from -1 to 4095, as said below
- weight_one: float32 [3, 3, 3, 64, 64], replicated, may hold values from -0.25 to 0.25
- bias_one: float32 [64], replicated, may hold values from -3 to 3
Outputs:
- block_out: float32 [4096, 64, 512], P(('gx', 'gy'))
Inputs may be any that keep to these rules, and one draw needn't show every extreme that they name: `send_pick`: entry j of a source device's row names the source row (0 to 15) sent to owner gx index j // 2 in place j % 2, or -1 for nothing; every source row is named exactly once; a source sends only to owners with its own gy index, at most 2 bricks to one owner; in every gy column some owner receives 2 bricks from every source. `occupancy`: 1 where a voxel of an owner brick slot is occupied; slots that receive no brick are all 0. Entry d of a slot is the global slot (owner rank times 32 plus slot) of the brick beside it across its -x, +x, -y, +y, -z or +z face, or -1; the relation is mutual; -y, +y, -z and +z neighbours have the same owner; -x and +x neighbours have the same owner or the owner of rank one lower (-x) or one higher (+x); empty slots have no neighbours and are no one's neighbour.
All inputs are finite; a program needn't handle non-finite values.
Results may differ from a plain program's by a relative error of at most 0.000062.
Values sent between devices are 32-bit elements; how exact they have to be, the bound alone decides.
No kernel may reach another device: no remote copies, remote signals or barrier semaphores. Data moves between devices by JAX's collectives and lax.ppermute only.
A program may use at most 128 MiB of HBM per device.

v0:
```python
import jax
import jax.numpy as jnp
from jax import lax
from jax.experimental import pallas as pl
from jax.experimental.pallas import tpu as pltpu
from jax.sharding import PartitionSpec as P


F32 = jnp.float32
BF16 = jnp.bfloat16
SLOTS = 32
SRC = 16
ROWS = 8 * SLOTS
GRANT = 67043328
PACK = 8
PLANE = 16


def passed_along(block, axis, distance):
    devices = range(lax.axis_size(axis))
    route = [(i - distance, i) for i in devices if i - distance in devices]
    return lax.ppermute(block, axis, route)


def lane_ids(shape):
    return lax.broadcasted_iota(jnp.int32, shape, len(shape) - 1)


def split(v):
    hi = v.astype(BF16)
    return hi, (v - hi.astype(F32)).astype(BF16)


def turned(x_ref, r, channels):
    low = lane_ids((32, 128)) < 64
    groups = []
    for g in range(4):
        p = g // 2
        a = x_ref[r, channels, p * 128 : (p + 1) * 128]
        b = x_ref[r, channels, (p + 2) * 128 : (p + 3) * 128]
        if g % 2 == 0:
            groups.append(jnp.where(low, a, pltpu.roll(b, 64, 1)))
        else:
            groups.append(jnp.where(low, pltpu.roll(a, 64, 1), b))
    return jnp.concatenate(groups, axis=0).T


def pack_first(x_ref, t_ref):
    channels = slice(32, 64)
    low = lane_ids((32, 128)) < 64
    group = lane_ids((8, 128)) // 32
    for first in range(0, PACK, 4):
        both = []
        for r in range(first, first + 4):
            t_ref[r, :128] = turned(x_ref, r, slice(0, 32))
            both.append(
                jnp.where(low, x_ref[r, channels, :128], x_ref[r, channels, 384:])
            )
        planes_t = jnp.concatenate(both, axis=0).T
        for r in range(4):
            for plane in range(2):
                for q in range(2):
                    value = None
                    for g in range(4):
                        at = (1 - plane) * 64 + (4 * q + g) * 8
                        to = (g + 3) % 4 if plane == 0 else g
                        tile = planes_t[at : at + 8]
                        if to != r:
                            tile = pltpu.roll(tile, (32 * (to - r)) % 128, 1)
                        if value is not None:
                            tile = jnp.where(group == to, tile, value)
                        value = tile
                    at = 128 + (2 * plane + q) * 8
                    t_ref[first + r, at : at + 8] = value


def pack_second(x_ref, t_ref):
    group = lane_ids((64, 128)) // 32
    group_b = lane_ids((32, 128)) // 32
    inner = (group_b == 1) | (group_b == 2)
    for r in range(PACK):
        t = turned(x_ref, r, slice(32, 64))
        t_ref[r, :64] = jnp.where(group == 0, t[64:], t[:64])
        t_ref[r, 64:96] = jnp.where(inner, t[64:96], pltpu.roll(t[96:], 64, 1))


def pack_kernel(half, pick_ref, x_ref, *refs):
    out_ref, t_ref, slot_ref, sem = refs[-4:]
    n = pl.program_id(0)

    @pl.when(n == 0)
    def _():
        for j in range(SLOTS):
            p = pick_ref[0, j]
            slot_ref[jnp.where(p < 0, SRC, p)] = j

    (pack_second if half else pack_first)(x_ref, t_ref.at[pl.ds(PACK * n, PACK)])

    def copy(r):
        return pltpu.make_async_copy(t_ref.at[r], out_ref.at[slot_ref[r]], sem.at[r])

    for r in range(PACK):
        copy(PACK * n + r).start()

    @pl.when(n == SRC // PACK - 1)
    def _():
        for r in range(SRC):
            copy(r).wait()


def pack(half, send_pick, features, after):
    rows = 96 if half else 160
    return pl.pallas_call(
        lambda *refs: pack_kernel(half, *refs),
        out_shape=jax.ShapeDtypeStruct((SLOTS, rows, 128), F32),
        grid=(SRC // PACK,),
        in_specs=[
            pl.BlockSpec(memory_space=pltpu.SMEM),
            pl.BlockSpec((PACK, 64, 512), lambda n: (n, 0, 0)),
        ]
        + [pl.BlockSpec(memory_space=pl.ANY)] * len(after),
        out_specs=pl.BlockSpec(memory_space=pl.ANY),
        scratch_shapes=[
            pltpu.VMEM((SRC, rows, 128), F32),
            pltpu.SMEM((SLOTS,), jnp.int32),
            pltpu.SemaphoreType.DMA((SRC,)),
        ],
        compiler_params=pltpu.CompilerParams(vmem_limit_bytes=GRANT),
        cost_estimate=pl.CostEstimate(
            flops=0, bytes_accessed=6 * 2**20, transcendentals=0
        ),
    )(send_pick, features, *after)


def masked(r_ref, m_ref, at, tile):
    rows = jnp.where(m_ref[at, tile] > 0, r_ref[at, tile], 0.0)
    return rows.reshape(rows.shape[0] * 8, 128)


def tile_rows(v_ref, tile):
    return v_ref[:, tile].reshape(ROWS, 128)


def planes_kernel(r_ref, m_ref, v_ref, up_ref, down_ref):
    group = lane_ids((32, 128)) // 32

    for c in range(PLANE // 4):
        bricks = slice(c * 4, c * 4 + 4)
        out = slice(c * 32, c * 32 + 32)
        for q in range(2):
            up = jnp.zeros((32, 128), F32)
            down = jnp.zeros((32, 128), F32)
            for g in range(4):
                tile = 4 * q + g
                v0 = masked(r_ref, m_ref, bricks, tile)
                v1 = masked(r_ref, m_ref, bricks, tile + 8)
                v_ref[bricks, tile] = v0.reshape(4, 8, 128)
                v_ref[bricks, tile + 8] = v1.reshape(4, 8, 128)
                v0 = pltpu.roll(v0, 32 * g, 1) if g else v0
                v1 = pltpu.roll(v1, 32 * g, 1) if g else v1
                up = jnp.where(group == (g + 3) % 4, v1, up)
                down = jnp.where(group == g, v0, down)
            up_ref[0, q, out, :] = up
            down_ref[0, q, out, :] = down
            up_ref[1, q, out, :] = masked(r_ref, m_ref, bricks, 16 + q)
            down_ref[1, q, out, :] = masked(r_ref, m_ref, bricks, 18 + q)


def planes(rows, mask_rows):
    shape = jax.ShapeDtypeStruct((2, 2, ROWS, 128), F32)
    tiles = pl.BlockSpec((PLANE, 20, 8, 128), lambda n: (n, 0, 0, 0))
    brick = pl.BlockSpec((PLANE, 16, 8, 128), lambda n: (n, 0, 0, 0))
    plane = pl.BlockSpec((2, 2, 8 * PLANE, 128), lambda n: (0, 0, n, 0))
    return pl.pallas_call(
        planes_kernel,
        out_shape=(jax.ShapeDtypeStruct((SLOTS, 16, 8, 128), F32), shape, shape),
        grid=(SLOTS // PLANE,),
        in_specs=[tiles, tiles],
        out_specs=(brick, plane, plane),
        name="planes",
        compiler_params=pltpu.CompilerParams(vmem_limit_bytes=GRANT),
        cost_estimate=pl.CostEstimate(
            flops=2**20, bytes_accessed=8 * 2**20, transcendentals=0
        ),
    )(rows, mask_rows)


def order_tables(order_ref):
    row = lax.broadcasted_iota(jnp.int32, (ROWS, ROWS), 0)
    column = lane_ids((ROWS, ROWS))
    forth = (((row & 31) << 3) | (row >> 5)) == column
    back = (((row & 7) << 5) | (row >> 3)) == column
    order_ref[0] = forth.astype(F32).astype(BF16)
    order_ref[1] = back.astype(F32).astype(BF16)


def moved_rows(order, value):
    both = jnp.concatenate(split(value), axis=1)
    return jnp.dot(order, both, preferred_element_type=F32)


def sides(p_ref, f_hi, f_lo):
    def spread(which, sources, targets):
        blocks = [f[y, z] for f in (f_hi, f_lo) for y, z in sources]
        moved = jnp.dot(
            p_ref[which], jnp.concatenate(blocks, axis=1), preferred_element_type=F32
        )
        n = 0
        for f in (f_hi, f_lo):
            for y, z in targets:
                f[y, z] = moved[:, n * 128 : (n + 1) * 128].astype(BF16)
                n += 1

    inner = range(1, 9)
    spread(0, [(8, z) for z in inner], [(0, z) for z in inner])
    spread(1, [(1, z) for z in inner], [(9, z) for z in inner])
    spread(2, [(y, 8) for y in range(10)], [(y, 0) for y in range(10)])
    spread(3, [(y, 1) for y in range(10)], [(y, 9) for y in range(10)])


def put(f_hi, f_lo, y, hi, lo):
    f_hi[y + 1, 1:9] = hi.astype(BF16).reshape(8, SLOTS, 128)
    f_lo[y + 1, 1:9] = lo.astype(BF16).reshape(8, SLOTS, 128)


def fill_mid(i, v_ref, order_ref, f_hi, f_lo):
    upper = lane_ids((ROWS, 128)) < 32 + 64 * i

    def one(y, carry):
        v0 = tile_rows(v_ref, y)
        v1 = tile_rows(v_ref, 8 + y)
        moved = moved_rows(order_ref[0], jnp.where(upper, v1, v0))
        put(f_hi, f_lo, y, moved[:, :128], moved[:, 128:])
        return carry

    lax.fori_loop(0, 8, one, 0, unroll=8)


def fill_ends(i, v_ref, px_ref, up, down, low, high, order_ref, halo, f_hi, f_lo):
    outer = lane_ids((ROWS, 128)) // 32 == 3 - 3 * i
    for q in range(2):
        near = jnp.where(i == 0, up[0, q], down[0, q])
        far = jnp.where(i == 0, low[0, q], high[0, q])
        halo[q] = moved_rows(px_ref[0], jnp.concatenate([near, far], axis=0))

    def one(q, carry):
        for g in range(4):
            y = q * 4 + g
            moved = moved_rows(order_ref[0], tile_rows(v_ref, 8 * i + y))
            parts = []
            for part in range(2):
                side = halo[q, :, 128 * part : 128 * part + 128]
                side = pltpu.roll(side, 128 - 32 * g, 1) if g else side
                parts.append(
                    jnp.where(outer, side, moved[:, 128 * part : 128 * part + 128])
                )
            put(f_hi, f_lo, y, *parts)
        return carry

    lax.fori_loop(0, 2, one, 0, unroll=2)


def inner_rows(m, y, r_ref, m_ref):
    group = lane_ids((ROWS, 128)) // 32
    every = slice(None)
    a = masked(r_ref, m_ref, every, y)
    b = masked(r_ref, m_ref, every, 8 + y % 4)
    b = pltpu.roll(b, 64, 1) if y > 3 else b
    return jnp.where((m >= 2) & ((group == 1) | (group == 2)), b, a)


def fill_inner(m, r_ref, m_ref, order_ref, f_hi, f_lo):
    for y in range(8):
        moved = moved_rows(order_ref[0], inner_rows(m, y, r_ref, m_ref))
        put(f_hi, f_lo, y, moved[:, :128], moved[:, 128:])


def fill_outer(m, r_ref, m_ref, px_ref, up, down, low, high, order_ref, halo, f_hi, f_lo):
    group = lane_ids((ROWS, 128)) // 32
    outer = group == jnp.where(m == 0, 3, 0)
    edge = group == jnp.where(m == 0, 0, 3)
    for q in range(2):
        own = jnp.where(m == 0, down[0, q], up[0, q])
        near = jnp.where(m == 0, up[0, q], down[0, q])
        far = jnp.where(m == 0, low[0, q], high[0, q])
        halo[q] = moved_rows(px_ref[0], jnp.concatenate([near, far], axis=0))
        halo[2 + q] = moved_rows(order_ref[0], own)
    for y in range(8):
        q, g = y // 4, y % 4
        moved = moved_rows(order_ref[0], inner_rows(m, y, r_ref, m_ref))
        parts = []
        for part in range(2):
            lanes = slice(128 * part, 128 * part + 128)
            side, own = halo[q, :, lanes], halo[2 + q, :, lanes]
            if g:
                side = pltpu.roll(side, 128 - 32 * g, 1)
                own = pltpu.roll(own, 128 - 32 * g, 1)
            value = jnp.where(outer, side, moved[:, lanes])
            parts.append(jnp.where(edge, own, value))
        put(f_hi, f_lo, y, *parts)


def convolve(f_hi, f_lo, w_ref, store, beside=lambda t: None):
    for t in range(4):
        parts = []
        for j in range(3):
            for k in range(3):
                for f in (f_hi, f_lo):
                    rows = f[2 * t + j : 2 * t + j + 2, k : k + 8]
                    parts.append(rows.reshape(2 * ROWS, 128))
        both = jnp.dot(
            jnp.concatenate(parts, axis=1), w_ref[0, 0], preferred_element_type=F32
        )
        beside(t)
        for d in range(2):
            at = slice(d * ROWS, (d + 1) * ROWS)
            store(2 * t + d, both[at, :128] + both[at, 128:])


def by_brick(order_ref, sum_ref, acc_ref):
    for y in range(8):
        back = moved_rows(order_ref[1], sum_ref[y * ROWS : (y + 1) * ROWS, :])
        acc_ref[:, y] = (back[:, :128] + back[:, 128:]).reshape(SLOTS, 8, 128)


def finish_pair(n, acc_ref, occ_ref, bias, out_ref):
    low = lane_ids((64, 128)) < 64
    b = 2 * n
    t = acc_ref[b : b + 2].reshape(128, 128).T
    even, odd = t[:64], t[64:]
    first = jnp.where(low, even, pltpu.roll(odd, 64, 1))
    second = jnp.where(low, pltpu.roll(even, 64, 1), odd)
    for d, value in enumerate((first, second)):
        mask = occ_ref[b + d : b + d + 1, :].astype(F32)
        out_ref[b + d] = mask * jnp.maximum(value + bias, 0.0)


def early_body(mid, refs):
    i = pl.program_id(0)
    v_ref, p_ref, w_ref, *refs = refs
    extra = []
    if not mid:
        extra, refs = refs[:5], refs[5:]
    out_ref, f_hi, f_lo, order_ref, halo = refs

    @pl.when(i == 0)
    def _():
        order_tables(order_ref)

    if mid:
        fill_mid(i, v_ref, order_ref, f_hi, f_lo)
    else:
        fill_ends(i, v_ref, *extra, order_ref, halo, f_hi, f_lo)
    sides(p_ref, f_hi, f_lo)

    def store(y, value):
        out_ref[0, y * ROWS : (y + 1) * ROWS, :] = value

    convolve(f_hi, f_lo, w_ref, store)


def late_body(*refs):
    r_ref, m_ref, p_ref, w_ref, *refs = refs
    sides_refs, refs = refs[:5], refs[5:]
    acc_mid, acc_ends, occ_ref, bias_ref, out_ref, *refs = refs
    f_hi, f_lo, order_ref, halo, sum_ref, acc_ref = refs
    m = pl.program_id(0)
    mid = (m == 1) | (m == 2)

    @pl.when(m == 0)
    def _():
        order_tables(order_ref)

    @pl.when(mid)
    def _():
        fill_inner(m, r_ref, m_ref, order_ref, f_hi, f_lo)

    @pl.when((m == 0) | (m == 3))
    def _():
        fill_outer(m, r_ref, m_ref, *sides_refs, order_ref, halo, f_hi, f_lo)

    def store(y, value):
        at = slice(y * ROWS, (y + 1) * ROWS)
        sum_ref[at, :] = value + jnp.where(mid, acc_mid[0, at, :], acc_ends[0, at, :])

    def before(t):
        bias = bias_ref[...]
        for n in range(4 * t, 4 * t + 4):
            finish_pair(n, acc_ref, occ_ref, bias, out_ref)

    @pl.when(m < 4)
    def _():
        sides(p_ref, f_hi, f_lo)
        convolve(f_hi, f_lo, w_ref, store, before)
        by_brick(order_ref, sum_ref, acc_ref)

    @pl.when(m == 4)
    def _():
        for t in range(4):
            before(t)


VMEM = pl.BlockSpec(memory_space=pltpu.VMEM)
FIELDS = [pltpu.VMEM((10, 10, SLOTS, 128), BF16)] * 2 + [pltpu.VMEM((2, ROWS, ROWS), BF16)]
PARAMS = pltpu.CompilerParams(vmem_limit_bytes=GRANT)


def half_of(h):
    return pl.BlockSpec((1, 2, ROWS, 128), lambda i: (h, 0, 0, 0))


def early(mid, rows, perms, weights, ends=()):
    kind = (lambda i: 1 - i) if mid else (lambda i: i)
    operands = [rows, perms, weights]
    specs = [VMEM, VMEM, pl.BlockSpec((1, 1, 18 * 128, 256), lambda i: (0, kind(i), 0, 0))]
    if not mid:
        operands += list(ends)
        specs += [pl.BlockSpec((1, ROWS, 2 * ROWS), lambda i: (i, 0, 0))] + [half_of(0)] * 4
    return pl.pallas_call(
        lambda *refs: early_body(mid, refs),
        out_shape=jax.ShapeDtypeStruct((2, 64 * SLOTS, 128), F32),
        grid=(2,),
        in_specs=specs,
        out_specs=pl.BlockSpec((1, 64 * SLOTS, 128), lambda i: (i, 0, 0)),
        scratch_shapes=FIELDS + [pltpu.VMEM((2, ROWS, ROWS), F32)],
        compiler_params=PARAMS,
        name="mid" if mid else "ends",
        cost_estimate=pl.CostEstimate(
            flops=2 * 2 * 2048 * 2304 * 256, bytes_accessed=8 * 2**20, transcendentals=0
        ),
    )(*operands)


def late(rows, mask_rows, perms, weights, ends, kept_mid, kept_ends, occupancy, bias):
    acc = (1, 64 * SLOTS, 128)
    specs = [VMEM, VMEM, VMEM]
    specs += [pl.BlockSpec((1, 1, 18 * 128, 256), lambda m: (1, m % 2, 0, 0))]
    specs += [pl.BlockSpec((1, ROWS, 2 * ROWS), lambda m: (jnp.minimum(m // 2, 1), 0, 0))]
    specs += [half_of(1)] * 4
    specs += [pl.BlockSpec(acc, lambda m: (jnp.minimum(m // 2, 1), 0, 0))]
    specs += [pl.BlockSpec(acc, lambda m: (m // 3, 0, 0))]
    specs += [pl.BlockSpec((SLOTS, 128), lambda m: (0, jnp.maximum(m - 1, 0))), VMEM]
    return pl.pallas_call(
        lambda *refs: late_body(*refs),
        out_shape=jax.ShapeDtypeStruct((SLOTS, 64, 512), F32),
        grid=(5,),
        in_specs=specs,
        out_specs=pl.BlockSpec((SLOTS, 64, 128), lambda m: (0, 0, jnp.maximum(m - 1, 0))),
        scratch_shapes=FIELDS
        + [
            pltpu.VMEM((4, ROWS, ROWS), F32),
            pltpu.VMEM(acc[1:], F32),
            pltpu.VMEM((SLOTS, 8, 8, 128), F32),
        ],
        compiler_params=PARAMS,
        name="late",
        cost_estimate=pl.CostEstimate(
            flops=4 * 2 * 2048 * 2304 * 256, bytes_accessed=16 * 2**20, transcendentals=0
        ),
    )(rows, mask_rows, perms, weights, *ends, kept_mid, kept_ends, occupancy, bias)


def mask_kernel(occ_ref, first_ref, second_ref):
    group = lax.broadcasted_iota(jnp.int32, (8, 128), 0)
    spread = (lane_ids((8, 128)) // 32 == group).astype(F32)

    def one(b, carry):
        rows = jnp.dot(occ_ref[b].T, spread, preferred_element_type=F32)
        first_ref[b] = rows[:160].reshape(20, 8, 128)
        second_ref[b] = rows[160:].reshape(12, 8, 128)
        return carry

    lax.fori_loop(0, SLOTS, one, 0, unroll=2)


def mask_tables(occupancy):
    occ = occupancy.astype(F32).reshape(SLOTS, 8, 64)
    base = occ.reshape(SLOTS, 2, 4, 64).transpose(0, 2, 1, 3).reshape(SLOTS, 4, 128)
    faces = occ.reshape(SLOTS, 8, 2, 4, 8)
    up = jnp.roll(faces[:, 7].transpose(0, 2, 1, 3), 3, axis=1)
    down = faces[:, 0].transpose(0, 2, 1, 3)
    a = jnp.concatenate([occ[:, 4:5], occ[:, 1:4]], axis=1)
    b = jnp.stack(
        [occ[:, 6, 32:], occ[:, 5, :32], occ[:, 6, :32], occ[:, 5, 32:]], axis=1
    )
    packed = [base, up.reshape(SLOTS, 4, 16), down.reshape(SLOTS, 4, 16), a, b]
    packed = jnp.pad(jnp.concatenate(packed, axis=2), ((0, 0), (0, 4), (0, 0)))
    return pl.pallas_call(
        mask_kernel,
        out_shape=(
            jax.ShapeDtypeStruct((SLOTS, 20, 8, 128), F32),
            jax.ShapeDtypeStruct((SLOTS, 12, 8, 128), F32),
        ),
        name="masks",
        compiler_params=pltpu.CompilerParams(vmem_limit_bytes=GRANT),
        cost_estimate=pl.CostEstimate(
            flops=2**20, bytes_accessed=4 * 2**20, transcendentals=0
        ),
    )(packed)


def weight_kernel(w_ref, out_ref):
    h = pl.program_id(0)
    row = lax.broadcasted_iota(jnp.int32, (32, 128), 0) + 32 * h
    lanes = lane_ids((32, 128))
    low = lanes < 64
    eye = (lanes % 64 == row).astype(F32)
    zero = jnp.zeros((32, 128), F32)
    channels = pl.ds(pl.multiple_of(32 * h, 32), 32)
    for jk in range(9):
        taps = [w_ref[9 * i + jk, channels, :] for i in range(3)]
        if jk == 4:
            taps[1] = taps[1] + eye
        taps = taps + [zero]
        window = [split(jnp.where(low, taps[d], taps[d - 1])) for d in range(4)]
        for kind, order in enumerate(((1, 2, 3, 0), (3, 0, 1, 2))):
            hi = jnp.concatenate([window[d][0] for d in order], axis=0)
            lo = jnp.concatenate([window[d][1] for d in order], axis=0)
            at = 256 * jk
            out_ref[0, kind, at : at + 128, :128] = hi
            out_ref[0, kind, at : at + 128, 128:] = lo
            out_ref[0, kind, at + 128 : at + 256, :128] = lo
            out_ref[0, kind, at + 128 : at + 256, 128:] = hi


def weight_tables(weights):
    w = weights.reshape(27, 64, 64)
    return pl.pallas_call(
        weight_kernel,
        out_shape=jax.ShapeDtypeStruct((2, 2, 18 * 128, 256), BF16),
        grid=(2,),
        in_specs=[pl.BlockSpec(memory_space=pltpu.VMEM)],
        out_specs=pl.BlockSpec((1, 2, 18 * 128, 256), lambda h: (h, 0, 0, 0)),
        name="weights",
        compiler_params=pltpu.CompilerParams(vmem_limit_bytes=GRANT),
        cost_estimate=pl.CostEstimate(
            flops=2**20, bytes_accessed=6 * 2**20, transcendentals=0
        ),
    )(jnp.concatenate([w, w], axis=2))


def owner(receive, occupancy, neighbours, own_rank, weight_one, bias_one, shift):
    mask_first, mask_second = mask_tables(occupancy)
    tables = weight_tables(weight_one)
    bias = jnp.broadcast_to(bias_one[:, None], (64, 128))
    present = neighbours >= 0
    local = neighbours % SLOTS
    away = (neighbours // SLOTS != own_rank).astype(jnp.int32) * SLOTS
    ids = jnp.where(present, local, -1)
    slots = jnp.arange(SLOTS, dtype=jnp.int32)
    perms = (ids[:, 2:].T[:, :, None] == slots).astype(BF16)
    wide = jnp.where(present, local + away, -SLOTS * 8)[:, :2].T[:, None, :] * 8
    wide = wide + jnp.arange(8, dtype=jnp.int32)[:, None]
    places = jnp.arange(2 * ROWS, dtype=jnp.int32)
    perms_x = (wide.reshape(2, ROWS)[:, :, None] == places).astype(BF16)
    rows = receive(0, ()).reshape(SLOTS, 20, 8, 128)
    ready = (mask_first, mask_second, tables, perms, perms_x, bias)
    later = receive(1, ready).reshape(SLOTS, 12, 8, 128)
    rows, up, down = planes(rows, mask_first)
    ends = (perms_x, up, down, shift(up, 1), shift(down, -1))
    kept_mid = early(True, rows, perms, tables)
    kept_ends = early(False, rows, perms, tables, ends)
    return late(
        later, mask_second, perms, tables, ends, kept_mid, kept_ends, occupancy, bias
    )


def shards(features, send_pick, occupancy, neighbours, weight_one, bias_one):
    def receive(h, after):
        outgoing = pack(h, send_pick, features, after)
        return lax.all_to_all(outgoing, "gx", split_axis=0, concat_axis=0, tiled=True)

    def shift(block, distance):
        return passed_along(block, ("gx", "gy"), distance)

    own_rank = lax.axis_index(("gx", "gy"))
    return owner(
        receive,
        occupancy,
        neighbours,
        own_rank,
        weight_one,
        bias_one,
        shift,
    )


def solution(mesh):
    in_specs = (
        P(("gx", "gy"), None, None),
        P(("gx", "gy"), None),
        P(("gx", "gy"), None),
        P(("gx", "gy"), None),
        P(),
        P(),
    )
    out_specs = P(("gx", "gy"), None, None)
    return jax.shard_map(
        shards, mesh=mesh, in_specs=in_specs, out_specs=out_specs, check_vma=False
    )
```

profile of v0, /device:TPU:24, one launch (start us, length us, event | category | flops | bytes accessed | tf_op | source)
XLA Modules:
  0.0 108.8 jit_solution(7352045211921382764)
XLA Ops:
  0.0 3.7 %shard_map.65 = f32[32,160,128]{2,1,0:T(8,128)} custom-call(s32[1,32]{1,0:T(1,128)} %refs_0_.3, f32[16,64,512]{2,1,0:T(8,128)} %refs_1_.3), custom_call_target="tpu_custom_call" | custom-call | bytes 6291456 | tf_op jit(solution)/shard_map/pallas_call | solution.py:113
  3.7 8.3 %all-to-all-start.1 = ((f32[32,160,128]{2,1,0:T(8,128)}), f32[32,160,128]{2,1,0:T(8,128)}, u32[]{:S(2)}, u32[]{:S(2)}) async-start(f32[32,160,128]{2,1,0:T(8,128)} %shard_map.65), calls=%async_computation.1 | async-start | bytes 5242880 | tf_op jit(solution)/shard_map/all_to_all | solution.py:571
  12.3 0.6 add.44
  12.9 0.6 add_select_fusion.2
  13.5 0.7 add.42
  15.2 0.2 concatenate.15
  15.5 0.7 pad.4.occ_ref
  16.2 1.2 %pad_maximum_fusion.w_ref = f32[27,64,128]{2,1,0:T(8,128)} fusion(f32[27,64,64]{2,1,0:T(8,128)S(1)} %bitcast.30), kind=kLoop, calls=%fused_computation.2 | loop fusion | flops 221184 | bytes 1327104 | tf_op jit(solution)/shard_map/concatenate | solution.py:539
  17.4 3.6 %weights.1.refs_4_.refs_2_.refs_3_ = bf16[2,2,2304,256]{3,2,1,0:T(8,128)(2,1)} custom-call(f32[27,64,128]{2,1,0:T(8,128)} %pad_maximum_fusion.w_ref), custom_call_target="tpu_custom_call" | custom-call | flops 1048576 | bytes 6291456 | tf_op jit(solution)/shard_map/weights/pallas_call | solution.py:528
  21.0 7.2 %masks.1 = (f32[32,20,8,128]{3,2,1,0:T(8,128)}, f32[32,12,8,128]{3,2,1,0:T(8,128)}) custom-call(f32[32,8,256]{2,1,0:T(8,128)} %pad.4.occ_ref), custom_call_target="tpu_custom_call" | custom-call | flops 1048576 | bytes 4194304 | tf_op jit(solution)/shard_map/masks/pallas_call | solution.py:488
  28.3 0.7 broadcast_add_fusion
  28.9 0.7 slice_bitcast_fusion.2
  29.6 0.7 fusion.1.refs_5_.refs_1_.refs_2_
  30.3 1.0 fusion.refs_6_.refs_3_.refs_4_
  31.3 1.3 %broadcast_in_dim.19.refs_7_.refs_12_ = f32[64,128]{1,0:T(8,128)} broadcast(f32[64]{0:T(128)} %param.11), dimensions={0} | broadcast | bytes 33024 | tf_op jit(solution)/shard_map/broadcast_in_dim | solution.py:545
  32.6 4.1 %shard_map.64 = f32[32,96,128]{2,1,0:T(8,128)} custom-call(s32[1,32]{1,0:T(1,128)} %refs_0_.3, f32[16,64,512]{2,1,0:T(8,128)} %refs_1_.3, f32[32,20,8,128]{3,2,1,0:T(8,128)} %get-tuple-element.10.refs_2_.m_ref, f32[32,12,8,128]{3,2,1,0:T(8,128)} %get-tuple-element.11.refs_3_.refs_1_, bf16[2,2,2304,256]{3,2,1,0:T(8,128)(2,1)} %weights.1.refs_4_.refs_2_.refs_3_, ...), custom_call_target="tpu_custom_call" | custom-call | bytes 6291456 | tf_op jit(solution)/shard_map/pallas_call | solution.py:113
  36.7 9.4 %all-to-all-done.1 = f32[32,160,128]{2,1,0:T(8,128)} async-done(((f32[32,160,128]{2,1,0:T(8,128)}), f32[32,160,128]{2,1,0:T(8,128)}, u32[]{:S(2)}, u32[]{:S(2)}) %all-to-all-start.1) | async-done | bytes 2621472 | tf_op jit(solution)/shard_map/all_to_all | solution.py:571
  46.1 7.4 %all-to-all-start = ((f32[32,96,128]{2,1,0:T(8,128)}), f32[32,96,128]{2,1,0:T(8,128)}, u32[]{:S(2)}, u32[]{:S(2)}) async-start(f32[32,96,128]{2,1,0:T(8,128)} %shard_map.64), calls=%async_computation | async-start | bytes 3145728 | tf_op jit(solution)/shard_map/all_to_all | solution.py:571
  53.5 3.9 %planes.1 = (f32[32,16,8,128]{3,2,1,0:T(8,128)}, f32[2,2,256,128]{3,2,1,0:T(8,128)}, f32[2,2,256,128]{3,2,1,0:T(8,128)}) custom-call(f32[32,20,8,128]{3,2,1,0:T(8,128)} %bitcast.15.r_ref, f32[32,20,8,128]{3,2,1,0:T(8,128)} %get-tuple-element.10.refs_2_.m_ref), custom_call_target="tpu_custom_call" | custom-call | flops 1048576 | bytes 8388608 | tf_op jit(solution)/shard_map/planes/pallas_call | solution.py:174
  57.4 1.9 %collective-permute-start = (f32[2,2,256,128]{3,2,1,0:T(8,128)}, f32[2,2,256,128]{3,2,1,0:T(8,128)}, u32[]{:S(2)}, u32[]{:S(2)}) collective-permute-start(f32[2,2,256,128]{3,2,1,0:T(8,128)} %get-tuple-element.12.refs_4_.refs_5_), channel_id=1, source_target_pairs={{0,1},{1,2},{2,3},{3,4},{4,5},{5,6},{6,7},{7,8},{8,9},{9,10},{10,1... | collective-permute-start | bytes 1572872 | tf_op jit(solution)/shard_map/ppermute | solution.py:22
  59.3 8.0 %collective-permute-start.1 = (f32[2,2,256,128]{3,2,1,0:T(8,128)}, f32[2,2,256,128]{3,2,1,0:T(8,128)}, u32[]{:S(2)}, u32[]{:S(2)}) collective-permute-start(f32[2,2,256,128]{3,2,1,0:T(8,128)} %get-tuple-element.13.refs_5_.refs_6_), channel_id=1, source_target_pairs={{1,0},{2,1},{3,2},{4,3},{5,4},{6,5},{7,6},{8,7},{9,8},{10,9},{11,1... | collective-permute-start | bytes 1572872 | tf_op jit(solution)/shard_map/ppermute | solution.py:22
  67.3 9.8 %mid.1.refs_9_ = f32[2,2048,128]{2,1,0:T(8,128)} custom-call(f32[32,16,8,128]{3,2,1,0:T(8,128)} %get-tuple-element.14.refs_0_, bf16[4,32,32]{2,1,0:T(8,128)(2,1)} %fusion.1.refs_5_.refs_1_.refs_2_, bf16[2,2,2304,256]{3,2,1,0:T(8,128)(2,1)} %weights.1.refs_4_.refs_2_.refs_3_), custom_call_target="tpu_custom_call" | custom-call | flops 4831838208 | bytes 8388608 | tf_op jit(solution)/shard_map/mid/pallas_call | solution.py:419
  77.1 10.4 %ends.1.refs_10_ = f32[2,2048,128]{2,1,0:T(8,128)} custom-call(f32[32,16,8,128]{3,2,1,0:T(8,128)} %get-tuple-element.14.refs_0_, bf16[4,32,32]{2,1,0:T(8,128)(2,1)} %fusion.1.refs_5_.refs_1_.refs_2_, bf16[2,2,2304,256]{3,2,1,0:T(8,128)(2,1)} %weights.1.refs_4_.refs_2_.refs_3_, bf16[2,256,512]{2,1,0:T(8,128)(2,1)} %fusion.refs_6_.refs_3_.refs_4_, ...), custom_call_target="tpu_custom_call" | custom-call | flops 4831838208 | bytes 8388608 | tf_op jit(solution)/shard_map/ends/pallas_call | solution.py:419
  87.5 21.3 %late.1 = f32[32,64,512]{2,1,0:T(8,128)} custom-call(f32[32,12,8,128]{3,2,1,0:T(8,128)} %bitcast.14.refs_0_, f32[32,12,8,128]{3,2,1,0:T(8,128)} %get-tuple-element.11.refs_3_.refs_1_, bf16[4,32,32]{2,1,0:T(8,128)(2,1)} %fusion.1.refs_5_.refs_1_.refs_2_, bf16[2,2,2304,256]{3,2,1,0:T(8,128)(2,1)} %weights.1.refs_4_.refs_2_.refs_3_, ...), custom_call_target="tpu_custom_call" | custom-call | flops 9663676416 | bytes 16777216 | tf_op jit(solution)/shard_map/late/pallas_call | solution.py:443
  (34 shorter events, 1.2 us)
Async XLA Ops:
  3.7 8.3 %copy-start.1 = (s32[32,512]{1,0:T(8,128)S(1)}, s32[32,512]{1,0:T(8,128)}, u32[]{:S(2)}) copy-start(s32[32,512]{1,0:T(8,128)} %refs_11_.1) | copy-start | bytes 196612
  3.7 9.2 %copy-start.2 = (s32[32,6]{0,1:T(8,128)S(1)}, s32[32,6]{0,1:T(8,128)}, u32[]{:S(2)}) copy-start(s32[32,6]{0,1:T(8,128)} %param.9) | copy-start | bytes 2308
  3.7 42.4 %all-to-all-start.1 = ((f32[32,160,128]{2,1,0:T(8,128)}), f32[32,160,128]{2,1,0:T(8,128)}, u32[]{:S(2)}, u32[]{:S(2)}) async-start(f32[32,160,128]{2,1,0:T(8,128)} %shard_map.65), calls=%async_computation.1 | async-start | bytes 5242880 | tf_op jit(solution)/shard_map/all_to_all | solution.py:571
  12.0 4.2 %copy-start = (f32[3,3,3,64,64]{4,3,2,1,0:T(8,128)S(1)}, f32[3,3,3,64,64]{4,3,2,1,0:T(8,128)}, u32[]{:S(2)}) copy-start(f32[3,3,3,64,64]{4,3,2,1,0:T(8,128)} %param.10) | copy-start | bytes 1327108
  46.1 41.4 %all-to-all-start = ((f32[32,96,128]{2,1,0:T(8,128)}), f32[32,96,128]{2,1,0:T(8,128)}, u32[]{:S(2)}, u32[]{:S(2)}) async-start(f32[32,96,128]{2,1,0:T(8,128)} %shard_map.64), calls=%async_computation | async-start | bytes 3145728 | tf_op jit(solution)/shard_map/all_to_all | solution.py:571
  57.4 19.7 %collective-permute-start = (f32[2,2,256,128]{3,2,1,0:T(8,128)}, f32[2,2,256,128]{3,2,1,0:T(8,128)}, u32[]{:S(2)}, u32[]{:S(2)}) collective-permute-start(f32[2,2,256,128]{3,2,1,0:T(8,128)} %get-tuple-element.12.refs_4_.refs_5_), channel_id=1, source_target_pairs={{0,1},{1,2},{2,3},{3,4},{4,5},{5,6},{6,7},{7,8},{8,9},{9,10},{10,1... | collective-permute-start | bytes 1572872 | tf_op jit(solution)/shard_map/ppermute | solution.py:22
  59.3 17.8 %collective-permute-start.1 = (f32[2,2,256,128]{3,2,1,0:T(8,128)}, f32[2,2,256,128]{3,2,1,0:T(8,128)}, u32[]{:S(2)}, u32[]{:S(2)}) collective-permute-start(f32[2,2,256,128]{3,2,1,0:T(8,128)} %get-tuple-element.13.refs_5_.refs_6_), channel_id=1, source_target_pairs={{1,0},{2,1},{3,2},{4,3},{5,4},{6,5},{7,6},{8,7},{9,8},{10,9},{11,1... | collective-permute-start | bytes 1572872 | tf_op jit(solution)/shard_map/ppermute | solution.py:22
where the time goes:
time: 111 us; the launch traced here: 109 us
  Pallas kernels  63.9 us (58%)
  starting transfers between devices  25.6 us (23%)
  waiting for transfers between devices  9.41 us (8%)
  local copies, waits for them, and re-layouts  5.33 us (5%)
  other arithmetic  4.31 us (4%)
    pallas_call x1, Pallas kernels, late(): pl.pallas_call(lambda *refs: late_body(*refs), out_shape=jax.ShapeDtypeSt...  21.3 us
    pallas_call x2, Pallas kernels, early(): pl.pallas_call(lambda *refs: early_body(mid, refs), out_shape=jax.ShapeDt...  20.2 us
    all_to_all x2, starting transfers between devices, receive(): lax.all_to_all(outgoing, 'gx', split_axis=0, concat_axis=0, tiled=True)  15.7 us
    ppermute x2, starting transfers between devices, passed_along(): return lax.ppermute(block, axis, route)  9.95 us
    all_to_all x2, waiting for transfers between devices, receive(): lax.all_to_all(outgoing, 'gx', split_axis=0, concat_axis=0, tiled=True)  9.41 us
    pallas_call x2, Pallas kernels, pack(): pl.pallas_call(lambda *refs: pack_kernel(half, *refs), out_shape=jax.Shap...  7.75 us
    pallas_call x1, Pallas kernels, mask_tables(): pl.pallas_call(mask_kernel, out_shape=(jax.ShapeDtypeStruct((SLOTS, 20, 8...  7.22 us
    pallas_call x1, Pallas kernels, planes(): pl.pallas_call(planes_kernel, out_shape=(jax.ShapeDtypeStruct((SLOTS, 16,...  3.86 us
  transfers between devices with their start and end apart: 4, of which 1 were waited for; matrix products, arithmetic and copies ran while one was open for 9% of the time, Pallas kernels for 36%

commit v1 on v0

--- a/solution.py
+++ b/solution.py
@@ -138,10 +138,10 @@
 
 
 def tile_rows(v_ref, tile):
-    return v_ref[:, tile].reshape(ROWS, 128)
-
-
-def planes_kernel(r_ref, m_ref, v_ref, up_ref, down_ref):
+    return masked(*v_ref, slice(None), tile)
+
+
+def planes_kernel(r_ref, m_ref, up_ref, down_ref):
     group = lane_ids((32, 128)) // 32
 
     for c in range(PLANE // 4):
@@ -152,31 +152,33 @@
             down = jnp.zeros((32, 128), F32)
             for g in range(4):
                 tile = 4 * q + g
-                v0 = masked(r_ref, m_ref, bricks, tile)
-                v1 = masked(r_ref, m_ref, bricks, tile + 8)
-                v_ref[bricks, tile] = v0.reshape(4, 8, 128)
-                v_ref[bricks, tile + 8] = v1.reshape(4, 8, 128)
+                v0 = r_ref[bricks, tile].reshape(32, 128)
+                v1 = r_ref[bricks, tile + 8].reshape(32, 128)
                 v0 = pltpu.roll(v0, 32 * g, 1) if g else v0
                 v1 = pltpu.roll(v1, 32 * g, 1) if g else v1
                 up = jnp.where(group == (g + 3) % 4, v1, up)
                 down = jnp.where(group == g, v0, down)
-            up_ref[0, q, out, :] = up
-            down_ref[0, q, out, :] = down
-            up_ref[1, q, out, :] = masked(r_ref, m_ref, bricks, 16 + q)
-            down_ref[1, q, out, :] = masked(r_ref, m_ref, bricks, 18 + q)
+            there = m_ref[bricks, q].reshape(32, 128) > 0
+            up_ref[0, q, out, :] = jnp.where(there, up, 0.0)
+            far = r_ref[bricks, 16 + q].reshape(32, 128)
+            up_ref[1, q, out, :] = jnp.where(there, far, 0.0)
+            there = m_ref[bricks, 2 + q].reshape(32, 128) > 0
+            down_ref[0, q, out, :] = jnp.where(there, down, 0.0)
+            far = r_ref[bricks, 18 + q].reshape(32, 128)
+            down_ref[1, q, out, :] = jnp.where(there, far, 0.0)
 
 
 def planes(rows, mask_rows):
     shape = jax.ShapeDtypeStruct((2, 2, ROWS, 128), F32)
     tiles = pl.BlockSpec((PLANE, 20, 8, 128), lambda n: (n, 0, 0, 0))
-    brick = pl.BlockSpec((PLANE, 16, 8, 128), lambda n: (n, 0, 0, 0))
+    faces = pl.BlockSpec((PLANE, 4, 8, 128), lambda n: (n, 4, 0, 0))
     plane = pl.BlockSpec((2, 2, 8 * PLANE, 128), lambda n: (0, 0, n, 0))
     return pl.pallas_call(
         planes_kernel,
-        out_shape=(jax.ShapeDtypeStruct((SLOTS, 16, 8, 128), F32), shape, shape),
+        out_shape=(shape, shape),
         grid=(SLOTS // PLANE,),
-        in_specs=[tiles, tiles],
-        out_specs=(brick, plane, plane),
+        in_specs=[tiles, faces],
+        out_specs=(plane, plane),
         name="planes",
         compiler_params=pltpu.CompilerParams(vmem_limit_bytes=GRANT),
         cost_estimate=pl.CostEstimate(
@@ -337,7 +339,8 @@
 
 def early_body(mid, refs):
     i = pl.program_id(0)
-    v_ref, p_ref, w_ref, *refs = refs
+    r_ref, m_ref, p_ref, w_ref, *refs = refs
+    v_ref = (r_ref, m_ref)
     extra = []
     if not mid:
         extra, refs = refs[:5], refs[5:]
@@ -409,10 +412,10 @@
     return pl.BlockSpec((1, 2, ROWS, 128), lambda i: (h, 0, 0, 0))
 
 
-def early(mid, rows, perms, weights, ends=()):
+def early(mid, rows, mask_rows, perms, weights, ends=()):
     kind = (lambda i: 1 - i) if mid else (lambda i: i)
-    operands = [rows, perms, weights]
-    specs = [VMEM, VMEM, pl.BlockSpec((1, 1, 18 * 128, 256), lambda i: (0, kind(i), 0, 0))]
+    operands = [rows, mask_rows, perms, weights]
+    specs = [VMEM] * 3 + [pl.BlockSpec((1, 1, 18 * 128, 256), lambda i: (0, kind(i), 0, 0))]
     if not mid:
         operands += list(ends)
         specs += [pl.BlockSpec((1, ROWS, 2 * ROWS), lambda i: (i, 0, 0))] + [half_of(0)] * 4
@@ -556,10 +559,10 @@
     rows = receive(0, ()).reshape(SLOTS, 20, 8, 128)
     ready = (mask_first, mask_second, tables, perms, perms_x, bias)
     later = receive(1, ready).reshape(SLOTS, 12, 8, 128)
-    rows, up, down = planes(rows, mask_first)
+    up, down = planes(rows, mask_first)
     ends = (perms_x, up, down, shift(up, 1), shift(down, -1))
-    kept_mid = early(True, rows, perms, tables)
-    kept_ends = early(False, rows, perms, tables, ends)
+    kept_mid = early(True, rows, mask_first, perms, tables)
+    kept_ends = early(False, rows, mask_first, perms, tables, ends)
     return late(
         later, mask_second, perms, tables, ends, kept_mid, kept_ends, occupancy, bias
     )

time: 111 us -> 112 us (level)
  Pallas kernels: 63.9 us -> 65.1 us
    pallas_call x2, Pallas kernels: 20.2 us -> 22.3 us  [early(): pl.pallas_call(lambda *refs: early_body(mid, refs), out_shape=jax.ShapeDt...]
  transfers between devices with their start and end apart: 4 -> 4, of which waited for: 1 -> 1; matrix products, arithmetic and copies ran while one was open for 9% -> 9% of each run, Pallas kernels for 36% -> 37%
where the time goes in v1:
time: 112 us; the launch traced here: 110 us
  Pallas kernels  65.1 us (58%)
  starting transfers between devices  25.6 us (23%)
  waiting for transfers between devices  9.4 us (8%)
  local copies, waits for them, and re-layouts  5.33 us (5%)
  other arithmetic  4.28 us (4%)
    pallas_call x2, Pallas kernels, early(): pl.pallas_call(lambda *refs: early_body(mid, refs), out_shape=jax.ShapeDt...  22.3 us
    pallas_call x1, Pallas kernels, late(): pl.pallas_call(lambda *refs: late_body(*refs), out_shape=jax.ShapeDtypeSt...  21.3 us
    all_to_all x2, starting transfers between devices, receive(): lax.all_to_all(outgoing, 'gx', split_axis=0, concat_axis=0, tiled=True)  15.7 us
    ppermute x2, starting transfers between devices, passed_along(): return lax.ppermute(block, axis, route)  9.95 us
    all_to_all x2, waiting for transfers between devices, receive(): lax.all_to_all(outgoing, 'gx', split_axis=0, concat_axis=0, tiled=True)  9.39 us
    pallas_call x2, Pallas kernels, pack(): pl.pallas_call(lambda *refs: pack_kernel(half, *refs), out_shape=jax.Shap...  7.74 us
    pallas_call x1, Pallas kernels, mask_tables(): pl.pallas_call(mask_kernel, out_shape=(jax.ShapeDtypeStruct((SLOTS, 20, 8...  7.28 us
    pallas_call x1, Pallas kernels, weight_tables(): pl.pallas_call(weight_kernel, out_shape=jax.ShapeDtypeStruct((2, 2, 18 *...  3.6 us
  transfers between devices with their start and end apart: 4, of which 1 were waited for; matrix products, arithmetic and copies ran while one was open for 9% of the time, Pallas kernels for 37%

profile of v1, /device:TPU:24, one launch (start us, length us, event | category | flops | bytes accessed | tf_op | source)
XLA Modules:
  0.0 109.9 jit_solution(5209719169487408922)
XLA Ops:
  0.0 3.7 %shard_map.65 = f32[32,160,128]{2,1,0:T(8,128)} custom-call(s32[1,32]{1,0:T(1,128)} %refs_0_.3, f32[16,64,512]{2,1,0:T(8,128)} %refs_1_.3), custom_call_target="tpu_custom_call" | custom-call | bytes 6291456 | tf_op jit(solution)/shard_map/pallas_call | solution.py:113
  3.7 8.3 %all-to-all-start.1 = ((f32[32,160,128]{2,1,0:T(8,128)}), f32[32,160,128]{2,1,0:T(8,128)}, u32[]{:S(2)}, u32[]{:S(2)}) async-start(f32[32,160,128]{2,1,0:T(8,128)} %shard_map.65), calls=%async_computation.1 | async-start | bytes 5242880 | tf_op jit(solution)/shard_map/all_to_all | solution.py:574
  12.3 0.6 add.44
  12.9 0.6 add_select_fusion.2
  13.5 0.7 add.42
  15.2 0.2 concatenate.15
  15.5 0.7 pad.4.occ_ref
  16.2 1.2 %pad_maximum_fusion.w_ref = f32[27,64,128]{2,1,0:T(8,128)} fusion(f32[27,64,64]{2,1,0:T(8,128)S(1)} %bitcast.30), kind=kLoop, calls=%fused_computation.2 | loop fusion | flops 221184 | bytes 1327104 | tf_op jit(solution)/shard_map/concatenate | solution.py:542
  17.4 3.6 %weights.1.refs_4_.refs_3_ = bf16[2,2,2304,256]{3,2,1,0:T(8,128)(2,1)} custom-call(f32[27,64,128]{2,1,0:T(8,128)} %pad_maximum_fusion.w_ref), custom_call_target="tpu_custom_call" | custom-call | flops 1048576 | bytes 6291456 | tf_op jit(solution)/shard_map/weights/pallas_call | solution.py:531
  21.0 7.3 %masks.1 = (f32[32,20,8,128]{3,2,1,0:T(8,128)}, f32[32,12,8,128]{3,2,1,0:T(8,128)}) custom-call(f32[32,8,256]{2,1,0:T(8,128)} %pad.4.occ_ref), custom_call_target="tpu_custom_call" | custom-call | flops 1048576 | bytes 4194304 | tf_op jit(solution)/shard_map/masks/pallas_call | solution.py:491
  28.3 0.7 broadcast_add_fusion
  29.0 0.7 slice_bitcast_fusion.2
  29.7 0.7 fusion.1.refs_5_.refs_2_
  30.4 1.0 fusion.refs_6_.refs_4_
  31.3 1.3 %broadcast_in_dim.19.refs_7_.refs_12_ = f32[64,128]{1,0:T(8,128)} broadcast(f32[64]{0:T(128)} %param.11), dimensions={0} | broadcast | bytes 33024 | tf_op jit(solution)/shard_map/broadcast_in_dim | solution.py:548
  32.7 4.1 %shard_map.64 = f32[32,96,128]{2,1,0:T(8,128)} custom-call(s32[1,32]{1,0:T(1,128)} %refs_0_.3, f32[16,64,512]{2,1,0:T(8,128)} %refs_1_.3, f32[32,20,8,128]{3,2,1,0:T(8,128)} %get-tuple-element.9.refs_2_.m_ref.refs_1_, f32[32,12,8,128]{3,2,1,0:T(8,128)} %get-tuple-element.10.refs_3_.refs_1_, bf16[2,2,2304,256]{3,2,1,0:T(8,128)(2,1)} %weights.1.refs_4_.refs_3_, ...), custom_call_target="tpu_custom_call" | custom-call | bytes 6291456 | tf_op jit(solution)/shard_map/pallas_call | solution.py:113
  36.7 9.4 %all-to-all-done.1 = f32[32,160,128]{2,1,0:T(8,128)} async-done(((f32[32,160,128]{2,1,0:T(8,128)}), f32[32,160,128]{2,1,0:T(8,128)}, u32[]{:S(2)}, u32[]{:S(2)}) %all-to-all-start.1) | async-done | bytes 2621472 | tf_op jit(solution)/shard_map/all_to_all | solution.py:574
  46.1 7.4 %all-to-all-start = ((f32[32,96,128]{2,1,0:T(8,128)}), f32[32,96,128]{2,1,0:T(8,128)}, u32[]{:S(2)}, u32[]{:S(2)}) async-start(f32[32,96,128]{2,1,0:T(8,128)} %shard_map.64), calls=%async_computation | async-start | bytes 3145728 | tf_op jit(solution)/shard_map/all_to_all | solution.py:574
  53.5 2.9 %planes.1 = (f32[2,2,256,128]{3,2,1,0:T(8,128)}, f32[2,2,256,128]{3,2,1,0:T(8,128)}) custom-call(f32[32,20,8,128]{3,2,1,0:T(8,128)} %bitcast.15.r_ref.refs_0_, f32[32,20,8,128]{3,2,1,0:T(8,128)} %get-tuple-element.9.refs_2_.m_ref.refs_1_), custom_call_target="tpu_custom_call" | custom-call | flops 1048576 | bytes 8388608 | tf_op jit(solution)/shard_map/planes/pallas_call | solution.py:176
  56.4 1.9 %collective-permute-start = (f32[2,2,256,128]{3,2,1,0:T(8,128)}, f32[2,2,256,128]{3,2,1,0:T(8,128)}, u32[]{:S(2)}, u32[]{:S(2)}) collective-permute-start(f32[2,2,256,128]{3,2,1,0:T(8,128)} %get-tuple-element.11.refs_5_), channel_id=1, source_target_pairs={{0,1},{1,2},{2,3},{3,4},{4,5},{5,6},{6,7},{7,8},{8,9},{9,10},{10,1... | collective-permute-start | bytes 1572872 | tf_op jit(solution)/shard_map/ppermute | solution.py:22
  58.3 8.0 %collective-permute-start.1 = (f32[2,2,256,128]{3,2,1,0:T(8,128)}, f32[2,2,256,128]{3,2,1,0:T(8,128)}, u32[]{:S(2)}, u32[]{:S(2)}) collective-permute-start(f32[2,2,256,128]{3,2,1,0:T(8,128)} %get-tuple-element.12.refs_6_), channel_id=1, source_target_pairs={{1,0},{2,1},{3,2},{4,3},{5,4},{6,5},{7,6},{8,7},{9,8},{10,9},{11,1... | collective-permute-start | bytes 1572872 | tf_op jit(solution)/shard_map/ppermute | solution.py:22
  66.4 10.9 %mid.1.refs_9_ = f32[2,2048,128]{2,1,0:T(8,128)} custom-call(f32[32,20,8,128]{3,2,1,0:T(8,128)} %bitcast.15.r_ref.refs_0_, f32[32,20,8,128]{3,2,1,0:T(8,128)} %get-tuple-element.9.refs_2_.m_ref.refs_1_, bf16[4,32,32]{2,1,0:T(8,128)(2,1)} %fusion.1.refs_5_.refs_2_, bf16[2,2,2304,256]{3,2,1,0:T(8,128)(2,1)} %weights.1.refs_4_.refs_3_), custom_call_target="tpu_custom_call" | custom-call | flops 4831838208 | bytes 8388608 | tf_op jit(solution)/shard_map/mid/pallas_call | solution.py:422
  77.3 11.4 %ends.1.refs_10_ = f32[2,2048,128]{2,1,0:T(8,128)} custom-call(f32[32,20,8,128]{3,2,1,0:T(8,128)} %bitcast.15.r_ref.refs_0_, f32[32,20,8,128]{3,2,1,0:T(8,128)} %get-tuple-element.9.refs_2_.m_ref.refs_1_, bf16[4,32,32]{2,1,0:T(8,128)(2,1)} %fusion.1.refs_5_.refs_2_, bf16[2,2,2304,256]{3,2,1,0:T(8,128)(2,1)} %weights.1.refs_4_.refs_3_, ...), custom_call_target="tpu_custom_call" | custom-call | flops 4831838208 | bytes 8388608 | tf_op jit(solution)/shard_map/ends/pallas_call | solution.py:422
  88.7 21.3 %late.1 = f32[32,64,512]{2,1,0:T(8,128)} custom-call(f32[32,12,8,128]{3,2,1,0:T(8,128)} %bitcast.14.refs_0_, f32[32,12,8,128]{3,2,1,0:T(8,128)} %get-tuple-element.10.refs_3_.refs_1_, bf16[4,32,32]{2,1,0:T(8,128)(2,1)} %fusion.1.refs_5_.refs_2_, bf16[2,2,2304,256]{3,2,1,0:T(8,128)(2,1)} %weights.1.refs_4_.refs_3_, bf16[2,256,512]{2,1,0:T(8,128)(2,1)} %fusion.refs_6_.refs_4_, ...), custom_call_target="tpu_custom_call" | custom-call | flops 9663676416 | bytes 16777216 | tf_op jit(solution)/shard_map/late/pallas_call | solution.py:446
  (34 shorter events, 1.2 us)
Async XLA Ops:
  3.7 8.3 %copy-start.1 = (s32[32,512]{1,0:T(8,128)S(1)}, s32[32,512]{1,0:T(8,128)}, u32[]{:S(2)}) copy-start(s32[32,512]{1,0:T(8,128)} %refs_11_.1) | copy-start | bytes 196612
  3.7 9.2 %copy-start.2 = (s32[32,6]{0,1:T(8,128)S(1)}, s32[32,6]{0,1:T(8,128)}, u32[]{:S(2)}) copy-start(s32[32,6]{0,1:T(8,128)} %param.9) | copy-start | bytes 2308
  3.7 42.4 %all-to-all-start.1 = ((f32[32,160,128]{2,1,0:T(8,128)}), f32[32,160,128]{2,1,0:T(8,128)}, u32[]{:S(2)}, u32[]{:S(2)}) async-start(f32[32,160,128]{2,1,0:T(8,128)} %shard_map.65), calls=%async_computation.1 | async-start | bytes 5242880 | tf_op jit(solution)/shard_map/all_to_all | solution.py:574
  12.0 4.2 %copy-start = (f32[3,3,3,64,64]{4,3,2,1,0:T(8,128)S(1)}, f32[3,3,3,64,64]{4,3,2,1,0:T(8,128)}, u32[]{:S(2)}) copy-start(f32[3,3,3,64,64]{4,3,2,1,0:T(8,128)} %param.10) | copy-start | bytes 1327108
  46.1 42.5 %all-to-all-start = ((f32[32,96,128]{2,1,0:T(8,128)}), f32[32,96,128]{2,1,0:T(8,128)}, u32[]{:S(2)}, u32[]{:S(2)}) async-start(f32[32,96,128]{2,1,0:T(8,128)} %shard_map.64), calls=%async_computation | async-start | bytes 3145728 | tf_op jit(solution)/shard_map/all_to_all | solution.py:574
  56.4 20.9 %collective-permute-start = (f32[2,2,256,128]{3,2,1,0:T(8,128)}, f32[2,2,256,128]{3,2,1,0:T(8,128)}, u32[]{:S(2)}, u32[]{:S(2)}) collective-permute-start(f32[2,2,256,128]{3,2,1,0:T(8,128)} %get-tuple-element.11.refs_5_), channel_id=1, source_target_pairs={{0,1},{1,2},{2,3},{3,4},{4,5},{5,6},{6,7},{7,8},{8,9},{9,10},{10,1... | collective-permute-start | bytes 1572872 | tf_op jit(solution)/shard_map/ppermute | solution.py:22
  58.3 19.0 %collective-permute-start.1 = (f32[2,2,256,128]{3,2,1,0:T(8,128)}, f32[2,2,256,128]{3,2,1,0:T(8,128)}, u32[]{:S(2)}, u32[]{:S(2)}) collective-permute-start(f32[2,2,256,128]{3,2,1,0:T(8,128)} %get-tuple-element.12.refs_6_), channel_id=1, source_target_pairs={{1,0},{2,1},{3,2},{4,3},{5,4},{6,5},{7,6},{8,7},{9,8},{10,9},{11,1... | collective-permute-start | bytes 1572872 | tf_op jit(solution)/shard_map/ppermute | solution.py:22
